TPU v7x, 512 devices: a whole 4x4x16 slice. The times are simulated.
512 devices in a mesh: seq: 32 (over z, core), mp: 16 (over y, x).
Axes of the slice: x: 4, y: 4, z: 16, core: 2. Of those that a mesh axis runs over, the one named last changes fastest.
Arguments:
- continued_prompt_entries: bfloat16 [4096, 4096], P('seq', 'mp'), may hold values from -6 to 6
- padded_prompt_entries: bfloat16 [4096, 4096], P('seq', 'mp'), may hold values from -6 to 6
- prompt_live_extents: int32 [64], P('seq'), may hold values from 8 to 64, as said below
- preceding_entry_line: bfloat16 [4096], P('mp'), may hold values from -6 to 6
- carried_memory: float32 [64, 64, 64], P('mp'), may hold values from -24 to 24
- token_mixing_ratios: float32 [5, 4096], replicated, may hold values from 0.05 to 0.95
- acceptance_transform: bfloat16 [4096, 4096], P('seq', 'mp'), may hold values from -0.09375 to 0.09375
- lookup_transform: bfloat16 [4096, 4096], P('seq', 'mp'), may hold values from -0.09375 to 0.09375
- payload_transform: bfloat16 [4096, 4096], P('seq', 'mp'), may hold values from -0.09375 to 0.09375
- gating_transform: bfloat16 [4096, 4096], P('seq', 'mp'), may hold values from -0.09375 to 0.09375
- fading_baseline: float32 [4096], P('mp'), may hold values from -10 to -3.5
- fading_left_factor: bfloat16 [4096, 128], replicated, may hold values from -0.09375 to 0.09375
- fading_right_factor: bfloat16 [128, 4096], P(None, 'mp'), may hold values from -0.5 to 0.5
- present_reward: float32 [64, 64], P('mp'), may hold values from -3 to 3
- group_layer_scaling: float32 [4096], P('mp'), may hold values from 0.5 to 1.5
- group_layer_shift_term: float32 [4096], P('mp'), may hold values from -1.8 to 1.8
- final_transform: bfloat16 [4096, 4096], P('mp', 'seq'), may hold values from -0.09375 to 0.09375
Outputs:
- mixed: bfloat16 [32, 256, 4096], P('seq', 'mp')
- span_states: float32 [32, 64, 64, 64], P('seq', 'mp')
- request_states: float32 [64, 64, 64, 64], P('seq', 'mp')
Inputs may be any that keep to these rules, and one draw needn't show every extreme that they name: `prompt_live_extents`: some request has all 64 rows live.
All inputs are finite; a program needn't handle non-finite values.
Results may differ from a plain program's by a relative error of at most 0.0076.
Values may be sent and summed in bfloat16 or wider, within the bound.
A program may use at most 64 MiB of HBM per device.

v0:
```python
import jax
import jax.numpy as jnp
from jax import lax
from jax.sharding import PartitionSpec as P

BLK = 64
norm_eps = 0.00064
highest = lax.Precision.HIGHEST


def passed_along(x, axis, by):
    length = lax.axis_size(axis)
    pairs = [(i, i + by) for i in range(length) if 0 <= i + by < length]
    return lax.ppermute(x, axis, pairs)


def entering(value, axis, join, neutral):
    count, mine = (lax.axis_size(axis), lax.axis_index(axis))
    pieces = jax.tree.map(lambda part: lax.all_gather(part, axis), value)
    total = jax.tree.map(
        lambda part, zero: jnp.full_like(part, 0) + jnp.asarray(zero, part.dtype), value, neutral
    )

    def hop(position, total):
        longer = join(total, jax.tree.map(lambda part: part[position], pieces))
        return jax.tree.map(lambda new, old: jnp.where(position < mine, new, old), longer, total)

    return lax.fori_loop(0, count - 1, hop, total)


def mix_rows(current, previous, weight):
    here = current.astype(jnp.float32)
    return (here + weight[None, :] * (previous.astype(jnp.float32) - here)).astype(jnp.bfloat16)


def block_sweep(
    evolving_memory,
    acceptance_entries,
    lookup_entries,
    payload_entries,
    log_fading_amount,
    diagonal_reward,
):
    inclusive = jnp.cumsum(log_fading_amount, axis=0)
    exclusive = inclusive - log_fading_amount
    recept_scaled = acceptance_entries * jnp.exp(exclusive)
    keys_scaled = lookup_entries * jnp.exp(-inclusive)
    scores = jnp.einsum("ihc,jhc->hij", recept_scaled, keys_scaled, precision=highest)
    count = acceptance_entries.shape[0]
    row_index = lax.broadcasted_iota(jnp.int32, (count, count), 0)
    col_index = lax.broadcasted_iota(jnp.int32, (count, count), 1)
    scores = jnp.where((row_index > col_index)[None], scores, 0.0)
    diagonal_contribution = jnp.sum(
        acceptance_entries * diagonal_reward[None] * lookup_entries, axis=-1, keepdims=True
    )
    answer_lines = (
        jnp.einsum("hij,jhd->ihd", scores, payload_entries, precision=highest)
        + diagonal_contribution * payload_entries
    )
    answer_lines = answer_lines + jnp.einsum(
        "ihc,hcd->ihd", recept_scaled, evolving_memory, precision=highest
    )
    total = inclusive[-1]
    carried = lookup_entries * jnp.exp(total[None] - inclusive)
    new_state = jnp.exp(total)[:, :, None] * evolving_memory + jnp.einsum(
        "jhc,jhd->hcd", carried, payload_entries, precision=highest
    )
    return (new_state, answer_lines)


def continued_recurrence(
    acceptance_entries, lookup_entries, payload_entries, log_fading_amount, diagonal_reward
):
    length, per_group_view, embedding_dimension = acceptance_entries.shape
    blocks = length // BLK

    def step(evolving_memory, entry_lines):
        return block_sweep(
            evolving_memory,
            entry_lines[0],
            entry_lines[1],
            entry_lines[2],
            entry_lines[3],
            diagonal_reward,
        )

    shaped = tuple(
        (
            a.reshape(blocks, BLK, per_group_view, embedding_dimension)
            for a in (acceptance_entries, lookup_entries, payload_entries, log_fading_amount)
        )
    )
    evolving_memory, results = lax.scan(
        step,
        jnp.zeros((per_group_view, embedding_dimension, embedding_dimension), jnp.float32),
        shaped,
    )
    return (evolving_memory, results.reshape(length, per_group_view, embedding_dimension))


def combine(earlier, later):
    return (earlier[0] + later[0], jnp.exp(later[0])[:, :, None] * earlier[1] + later[1])


def shifted_rows(current, edge_row, long_rows, requests, slot_rows):
    feature_part = current.shape[1]
    long_prev = jnp.concatenate([edge_row, current[: long_rows - 1]], axis=0)
    short_view = current[long_rows:].reshape(requests, slot_rows, feature_part)
    short_prev = jnp.concatenate(
        [jnp.zeros((requests, 1, feature_part), current.dtype), short_view[:, :-1]], axis=1
    )
    short_prev = short_prev.reshape(requests * slot_rows, feature_part)
    return jnp.concatenate([long_prev, short_prev], axis=0)


def on_device(
    continued_prompt_entries,
    padded_prompt_entries,
    prompt_live_extents,
    preceding_entry_line,
    carried_memory,
    token_mixing_ratios,
    acceptance_transform,
    lookup_transform,
    payload_transform,
    gating_transform,
    fading_baseline,
    fading_left_factor,
    fading_right_factor,
    present_reward,
    group_layer_scaling,
    group_layer_shift_term,
    final_transform,
):
    long_rows = continued_prompt_entries.shape[0]
    requests = prompt_live_extents.shape[0]
    slot_rows = padded_prompt_entries.shape[0] // requests
    per_group_view, embedding_dimension = present_reward.shape
    arrived = passed_along(continued_prompt_entries[-1:], "seq", 1)
    first = lax.axis_index("seq") == 0
    edge_row = jnp.where(first, preceding_entry_line[None, :], arrived)
    current = jnp.concatenate([continued_prompt_entries, padded_prompt_entries], axis=0)
    current, edge_full = (
        lax.all_gather(current, "mp", axis=1, tiled=True),
        lax.all_gather(edge_row, "mp", axis=1, tiled=True),
    )
    previous = shifted_rows(current, edge_full, long_rows, requests, slot_rows)
    mixes = [mix_rows(current, previous, token_mixing_ratios[index]) for index in range(5)]
    total_rows = current.shape[0]
    columns = acceptance_transform.shape[1]
    pieces = (
        lax.all_gather(acceptance_transform, "seq", axis=0, tiled=True),
        lax.all_gather(lookup_transform, "seq", axis=0, tiled=True),
        lax.all_gather(payload_transform, "seq", axis=0, tiled=True),
        lax.all_gather(gating_transform, "seq", axis=0, tiled=True),
    )
    acceptance_entries, lookup_entries, payload_entries, gate = tuple(
        (
            jnp.dot(source, piece, preferred_element_type=jnp.float32)
            for source, piece in zip(mixes[:4], pieces)
        )
    )
    squeezed = jnp.tanh(
        jnp.dot(mixes[4], fading_left_factor, preferred_element_type=jnp.float32)
    ).astype(jnp.bfloat16)
    log_fading_amount = -jnp.exp(
        fading_baseline[None, :]
        + jnp.dot(squeezed, fading_right_factor, preferred_element_type=jnp.float32)
    )
    recept3, keys3, values3, decay3 = [
        a.reshape(total_rows, per_group_view, embedding_dimension)
        for a in (acceptance_entries, lookup_entries, payload_entries, log_fading_amount)
    ]
    local_state, long_out = continued_recurrence(
        recept3[:long_rows],
        keys3[:long_rows],
        values3[:long_rows],
        decay3[:long_rows],
        present_reward,
    )
    long_decay = decay3[:long_rows]
    group_total = jnp.sum(long_decay, axis=0)
    blank = (
        jnp.zeros((per_group_view, embedding_dimension), jnp.float32),
        jnp.zeros((per_group_view, embedding_dimension, embedding_dimension), jnp.float32),
    )
    prefix_total, prefix_state = entering((group_total, local_state), "seq", combine, blank)
    incoming = jnp.exp(prefix_total)[:, :, None] * carried_memory + prefix_state
    before_row = jnp.cumsum(long_decay, axis=0) - long_decay
    long_out = long_out + jnp.einsum(
        "ihc,hcd->ihd", recept3[:long_rows] * jnp.exp(before_row), incoming, precision=highest
    )
    span_end = jnp.exp(group_total)[:, :, None] * incoming + local_state
    live_rows = (
        lax.broadcasted_iota(jnp.int32, (requests, slot_rows), 1) < prompt_live_extents[:, None]
    )
    live_flat = live_rows.reshape(requests * slot_rows).astype(jnp.float32)[:, None, None]
    short_shape = (requests, slot_rows, per_group_view, embedding_dimension)
    short_recept = recept3[long_rows:].reshape(short_shape)
    short_keys = (keys3[long_rows:] * live_flat).reshape(short_shape)
    short_values = values3[long_rows:].reshape(short_shape)
    short_decay = (decay3[long_rows:] * live_flat).reshape(short_shape)
    zeroed_memory = jnp.zeros(
        (per_group_view, embedding_dimension, embedding_dimension), jnp.float32
    )

    def request_pass(acceptance_lines, lookup_table, payload_table, fading_table):
        return block_sweep(
            zeroed_memory,
            acceptance_lines,
            lookup_table,
            payload_table,
            fading_table,
            present_reward,
        )

    request_states, short_out = jax.vmap(request_pass)(
        short_recept, short_keys, short_values, short_decay
    )
    wkv = jnp.concatenate(
        [long_out, short_out.reshape(requests * slot_rows, per_group_view, embedding_dimension)],
        axis=0,
    )
    mean = jnp.mean(wkv, axis=-1, keepdims=True)
    centred = wkv - mean
    variance = jnp.mean(centred * centred, axis=-1, keepdims=True)
    normed = (centred * lax.rsqrt(variance + norm_eps)).reshape(
        total_rows, columns
    ) * group_layer_scaling[None, :] + group_layer_shift_term[None, :]
    row_live = jnp.concatenate(
        [jnp.ones((long_rows,), dtype=bool), live_rows.reshape(requests * slot_rows)], axis=0
    )
    hidden = jnp.where(row_live[:, None], normed * jax.nn.silu(gate), 0.0).astype(jnp.bfloat16)
    full_out = lax.all_gather(final_transform, "seq", axis=1, tiled=True)
    mixed_rows = lax.psum_scatter(
        jnp.dot(hidden, full_out, preferred_element_type=jnp.float32),
        "mp",
        scatter_dimension=0,
        tiled=True,
    )
    return (mixed_rows.astype(jnp.bfloat16)[None], span_end[None], request_states)


def solution(mesh):
    placed = (
        P("seq", "mp"),
        P("seq", "mp"),
        P("seq"),
        P("mp"),
        P("mp", None, None),
        P(),
        P("seq", "mp"),
        P("seq", "mp"),
        P("seq", "mp"),
        P("seq", "mp"),
        P("mp"),
        P(),
        P(None, "mp"),
        P("mp", None),
        P("mp"),
        P("mp"),
        P("mp", "seq"),
    )
    return jax.shard_map(
        on_device,
        mesh=mesh,
        in_specs=placed,
        out_specs=(P("seq", "mp", None), P("seq", "mp", None, None), P("seq", "mp", None, None)),
        check_vma=False,
    )
```

profile of v0, /device:TPU:2, one launch (start us, length us, event | category | flops | bytes accessed | tf_op | source)
XLA Modules:
  0.0 631.1 jit_solution(9215683122175775181)
XLA Ops:
  7.2 1.6 pad_maximum_fusion.2
  11.7 1.7 collective-permute-start
  13.4 1.9 fusion.85
  16.0 27.3 %all_gather.34 = bf16[1,4096]{1,0:T(2,128)(2,1)} all-gather(bf16[1,256]{1,0:T(2,128)(2,1)S(1)} %broadcast_select_fusion), channel_id=1, replica_groups=mesh['seq'=32,'mp'=16] {'mp'}, dimensions={1}, use_global_device_ids=true | all-gather | bytes 8704 | tf_op jit(solution)/shard_map/all_gather | solution.py:145
  43.3 35.5 %all-gather.9.cloned.1.call-done = bf16[256,4096]{1,0:T(8,128)(2,1)} async-done(((bf16[256,256]{1,0:T(8,128)(2,1)}), bf16[256,4096]{1,0:T(8,128)(2,1)}) %all-gather.9.cloned.1.call-update) | async-done | bytes 2097168 | tf_op jit(solution)/shard_map/all_gather | solution.py:144
  78.7 1.5 slice.100
  80.2 1.2 concatenate.24
  81.4 1.1 slice.99
  82.5 3.0 fusion.41
  85.5 1.3 slice_reduce_fusion
  86.8 1.1 reshape.138
  87.9 64.6 %all-gather.15.cloned.1.call-done = bf16[4096,256]{1,0:T(8,128)(2,1)} async-done(((bf16[128,256]{1,0:T(8,128)(2,1)}), bf16[4096,256]{1,0:T(8,128)(2,1)}) %all-gather.15.cloned.1.call-update) | async-done | bytes 2097168 | tf_op jit(solution)/shard_map/all_gather | solution.py:152
  152.5 3.7 fusion.25
  157.0 66.3 %all-gather.11.cloned.1.call-done = bf16[4096,256]{1,0:T(8,128)(2,1)} async-done(((bf16[128,256]{1,0:T(8,128)(2,1)}), bf16[4096,256]{1,0:T(8,128)(2,1)}) %all-gather.11.cloned.1.call-update) | async-done | bytes 2097168 | tf_op jit(solution)/shard_map/all_gather | solution.py:153
  223.3 4.0 fusion.29
  228.2 65.8 %all-gather.13.cloned.1.call-done = bf16[4096,256]{1,0:T(8,128)(2,1)} async-done(((bf16[128,256]{1,0:T(8,128)(2,1)}), bf16[4096,256]{1,0:T(8,128)(2,1)}) %all-gather.13.cloned.1.call-update) | async-done | bytes 2097168 | tf_op jit(solution)/shard_map/all_gather | solution.py:154
  294.0 3.6 fusion.27
  298.5 13.3 %while.29 = (s32[]{:T(128)}, f32[4,64,64]{2,1,0:T(8,128)S(1)}, f32[2,64,4,64]{1,0,3,2:T(2,128)}, f32[2,64,4,64]{1,0,3,2:T(2,128)S(1)}, f32[2,64,4,64]{3,2,1,0:T(...) while((s32[]{:T(128)}, f32[4,64,64]{2,1,0:T(8,128)S(1)}, ...), condition=%wide.region_3.4_spmd.clone, body=%wide.region_0.3_spmd.clone.sunk | while | flops 51646208 | bytes 2444416 | solution.py:93
  300.4 4.3 dynamic_update_slice.6
  307.1 4.3 dynamic_update_slice.6
  314.7 32.2 %all_gather.39 = f32[32,4,64]{2,1,0:T(4,128)} all-gather(f32[1,4,64]{2,1,0:T(4,128)S(1)} %all_gather.38), channel_id=1, replica_groups=mesh['seq'=32,'mp'=16] {'seq'}, dimensions={0}, use_global_device_ids=true | all-gather | bytes 33792 | tf_op jit(solution)/shard_map/all_gather | solution.py:19
  347.6 1.2 reshape.144
  348.9 1.1 slice.94
  350.0 1.1 exponential_multiply_fusion
  351.2 1.1 reshape.143
  358.3 25.6 %all-gather.21.cloned.1.call-done = f32[128,64,64]{2,1,0:T(8,128)} async-done(((f32[4,64,64]{2,1,0:T(8,128)}), f32[128,64,64]{2,1,0:T(8,128)}) %all-gather.21.cloned.1.call-update) | async-done | bytes 2097168 | tf_op jit(solution)/shard_map/all_gather | solution.py:19
  383.9 53.9 %while.30 = (s32[]{:T(128)}, f32[4,64]{1,0:T(4,128)S(1)}, f32[4,64,64]{2,1,0:T(8,128)S(1)}, s32[]{:T(128)}, f32[32,4,64]{2,1,0:T(4,128)}, /*index=5*/f32[32,4,64,64]{3,2,1,0:T(8,128)}, s32[]{:T(128)}, s32[]{:T(128)}) while((s32[]{:T(128)}, f32[4,64]{1,0:T(4,128)S(1)}, f32[4,64,64]{2,1,0:T(8,128)S(1)}, s32[]{:T(128)}, ...), condition=%wide.region_6.7_spmd.clone, body=%wide.region_5.6_spmd.clone.sunk | while | flops 66308 | bytes 201843 | solution.py:28
  384.5 1.0 fusion.119
  386.2 1.0 fusion.119
  387.9 1.0 fusion.119
  400.2 1.0 fusion.119
  403.7 1.0 fusion.119
  405.4 1.0 fusion.119
  407.1 1.0 fusion.119
  408.9 1.0 fusion.119
  412.3 1.0 fusion.119
  422.7 1.0 fusion.119
  428.0 1.0 fusion.119
  437.8 1.8 fusion.42
  442.3 1.8 copy.102
  444.8 1.8 copy.101
  446.5 1.7 copy.99
  448.2 5.8 all-gather.17.cloned.1.call-done
  454.0 72.6 %all-gather.19.cloned.1.call-done = bf16[256,4096]{1,0:T(8,128)(2,1)} async-done(((bf16[256,128]{1,0:T(8,128)(2,1)}), bf16[256,4096]{1,0:T(8,128)(2,1)}) %all-gather.19.cloned.1.call-update) | async-done | bytes 2097168 | tf_op jit(solution)/shard_map/all_gather | solution.py:234
  526.5 7.5 %fusion.63 = f32[256,4096]{1,0:T(8,128)} fusion(bf16[256,4096]{1,0:T(8,128)(2,1)} %all-gather.19.cloned.1.call-done, f32[256,256]{1,0:T(8,128)} %copy.102, f32[256,256]{1,0:T(8,128)} %copy.101, f32[128,256]{1,0:T(8,128)} %concatenate.27, f32[128,256]{1,0:T(8,128)} %copy.99, bf16[4096,256]{1,0:T(8,128)(2,1)} %all-gather.17.cloned.1.call-done, ...), kind=kOutput, calls=%fused_computation.83 | convolution fusion | flops 1086062592 | bytes 13388032 | tf_op jit(solution)/shard_map/dot_general | solution.py:236
  535.0 1.3 convolution_add_fusion.1
  537.1 85.6 %reduce-scatter.2.cloned.1.call-done = f32[16,4096]{1,0:T(8,128)} async-done(((f32[256,4096]{1,0:T(8,128)}), f32[16,4096]{1,0:T(8,128)}) %reduce-scatter.2.cloned.1.call-update) | async-done | bytes 262160 | tf_op jit(solution)/shard_map/reduce_scatter | solution.py:235
  622.7 1.6 convert_bitcast_fusion
  (180 shorter events, 66.9 us)
Async XLA Ops:
  7.2 75.3 %copy-start = (bf16[4096,128]{1,0:T(8,128)(2,1)S(1)}, bf16[4096,128]{1,0:T(8,128)(2,1)}, u32[]{:S(2)}) copy-start(bf16[4096,128]{1,0:T(8,128)(2,1)} %param.32) | copy-start | bytes 3145732
  7.2 71.5 %all-gather.9.cloned.1.call-start = ((), (), s32[]{:S(2)}) async-start(), calls=%async_computation.1 | async-start | bytes 2228224 | tf_op jit(solution)/shard_map/all_gather | solution.py:144
  8.9 143.6 %all-gather.15.cloned.1.call-start = ((), (), s32[]{:S(2)}) async-start(), calls=%async_computation.4 | async-start | bytes 2162688 | tf_op jit(solution)/shard_map/all_gather | solution.py:152
  9.6 213.7 %all-gather.11.cloned.1.call-start = ((), (), s32[]{:S(2)}) async-start(), calls=%async_computation.2 | async-start | bytes 2162688 | tf_op jit(solution)/shard_map/all_gather | solution.py:153
  10.4 283.7 %all-gather.13.cloned.1.call-start = ((), (), s32[]{:S(2)}) async-start(), calls=%async_computation.3 | async-start | bytes 2162688 | tf_op jit(solution)/shard_map/all_gather | solution.py:154
  10.9 372.9 %all-gather.21.cloned.1.call-start = ((), (), s32[]{:S(2)}) async-start(), calls=%async_computation.8 | async-start | bytes 4325376 | tf_op jit(solution)/shard_map/all_gather | solution.py:19
  11.7 3.7 collective-permute-start
  78.7 2.7 copy-start.3
  223.3 70.7 %copy-start.8 = (bf16[2,64,4096]{2,1,0:T(8,128)(2,1)S(1)}, bf16[2,64,4096]{2,1,0:T(8,128)(2,1)}, u32[]{:S(2)}) copy-start(bf16[2,64,4096]{2,1,0:T(8,128)(2,1)} %concatenate.24) | copy-start | bytes 3145732
  223.3 70.7 %copy-start.14 = (bf16[1,4096]{1,0:T(2,128)(2,1)S(1)}, bf16[1,4096]{1,0:T(2,128)(2,1)}, u32[]{:S(2)}) copy-start(bf16[1,4096]{1,0:T(2,128)(2,1)} %all_gather.34) | copy-start | bytes 24580
  294.0 4.5 copy-start.13
  298.5 15.4 %copy-start.16 = (s32[2]{0:T(128)S(1)}, s32[2]{0:T(128)}, u32[]{:S(2)}) copy-start(s32[2]{0:T(128)} %param.23) | copy-start | bytes 28
  298.5 16.1 %copy-start.15 = (f32[256]{0:T(256)S(1)}, f32[256]{0:T(256)}, u32[]{:S(2)}) copy-start(f32[256]{0:T(256)} %get-tuple-element.272) | copy-start | bytes 3076
  298.5 48.3 %copy-start.6 = (f32[128,256]{0,1:T(8,128)S(1)}, f32[128,256]{0,1:T(8,128)}, u32[]{:S(2)}) copy-start(f32[128,256]{0,1:T(8,128)} %get-tuple-element.274) | copy-start | bytes 393220
  298.5 48.5 %copy-start.10 = (f32[128,256]{0,1:T(8,128)S(1)}, f32[128,256]{0,1:T(8,128)}, u32[]{:S(2)}) copy-start(f32[128,256]{0,1:T(8,128)} %get-tuple-element.273) | copy-start | bytes 393220
  311.8 0.7 copy-start.1
  312.5 141.5 %all-gather.17.cloned.1.call-start = ((), (), s32[]{:S(2)}) async-start(), calls=%async_computation.5 | async-start | bytes 2162688 | tf_op jit(solution)/shard_map/all_gather | solution.py:155
  313.0 213.5 %all-gather.19.cloned.1.call-start = ((), (), s32[]{:S(2)}) async-start(), calls=%async_computation.6 | async-start | bytes 2162688 | tf_op jit(solution)/shard_map/all_gather | solution.py:234
  313.8 308.9 %reduce-scatter.2.cloned.1.call-start = ((), (), s32[]{:S(2)}) async-start(), calls=%async_computation.7 | async-start | bytes 4456448 | tf_op jit(solution)/shard_map/reduce_scatter | solution.py:235
  347.3 7.4 %copy-start.12 = (f32[2,64,4,64]{1,0,3,2:T(2,128)S(1)}, f32[2,64,4,64]{1,0,3,2:T(2,128)}, u32[]{:S(2)}) copy-start(f32[2,64,4,64]{1,0,3,2:T(2,128)} %get-tuple-element.156) | copy-start | bytes 393220
  347.5 5.4 copy-start.7
  354.6 171.9 %copy-start.17 = (f32[256]{0:T(256)S(1)}, f32[256]{0:T(256)}, u32[]{:S(2)}) copy-start(f32[256]{0:T(256)} %param.36) | copy-start | bytes 3076
  358.3 168.2 %copy-start.4 = (bf16[256,4096]{1,0:T(8,128)(2,1)S(1)}, bf16[256,4096]{1,0:T(8,128)(2,1)}, u32[]{:S(2)}) copy-start(bf16[256,4096]{1,0:T(8,128)(2,1)} %all-gather.9.cloned.1.call-done) | copy-start | bytes 6291460
  439.6 1.0 copy-start.5
  534.0 0.9 copy-start.9
  534.0 2.3 copy-start.2
  534.0 2.3 copy-start.11
Sparse Core Ops, SparseCore 0:
  11.6 67.0 all-gather.8
  80.8 71.5 all-gather.14
  154.6 68.6 all-gather.10
  225.3 68.6 all-gather.12
  312.6 71.2 all-gather.20
  385.8 68.0 all-gather.16
  456.0 70.4 all-gather.18
  534.2 88.4 reduce-scatter.1
where the time goes:
time: 633 us; the launch traced here: 631 us
  waiting for transfers between devices  425 us (67%)
  other arithmetic  64.5 us (10%)
  blocking collectives  59.4 us (9%)
  local copies, waits for them, and re-layouts  35.3 us (6%)
  matrix products  29.4 us (5%)
  between operations  14.5 us (2%)
    reduce_scatter x1, waiting for transfers between devices, on_device(): lax.psum_scatter(jnp.dot(hidden, full_out, preferred_element_type=jnp.flo...  85.6 us
    all_gather x1, waiting for transfers between devices, on_device(): full_out = lax.all_gather(final_transform, 'seq', axis=1, tiled=True)  72.6 us
    all_gather x1, waiting for transfers between devices, on_device(): lax.all_gather(lookup_transform, 'seq', axis=0, tiled=True)  66.3 us
    all_gather x1, waiting for transfers between devices, on_device(): lax.all_gather(payload_transform, 'seq', axis=0, tiled=True)  65.8 us
    all_gather x1, waiting for transfers between devices, on_device(): lax.all_gather(acceptance_transform, 'seq', axis=0, tiled=True)  64.6 us
    all_gather x1, waiting for transfers between devices, on_device(): lax.all_gather(current, 'mp', axis=1, tiled=True)  35.5 us
    all_gather x1, blocking collectives, entering(): pieces = jax.tree.map(lambda part: lax.all_gather(part, axis), value)  32.2 us
    select_n x31, other arithmetic, hop(): jnp.where(position < mine, new, old)  32 us
  transfers between devices with their start and end apart: 9, of which 8 were waited for; matrix products, arithmetic and copies ran while one was open for 16% of the time, Pallas kernels for 0%

commit v1 on v0

--- a/solution.py
+++ b/solution.py
@@ -150,7 +150,10 @@
     columns = acceptance_transform.shape[1]
     pieces = (
         lax.all_gather(acceptance_transform, "seq", axis=0, tiled=True),
-        lax.all_gather(lookup_transform, "seq", axis=0, tiled=True),
+        jnp.concatenate(
+            lax.all_to_all(jnp.stack([lookup_transform] * lax.axis_size("seq")), "seq", 0, 0),
+            axis=0,
+        ),
         lax.all_gather(payload_transform, "seq", axis=0, tiled=True),
         lax.all_gather(gating_transform, "seq", axis=0, tiled=True),
     )

time: 633 us -> 576 us (0.910)
  waiting for transfers between devices: 425 us -> 359 us
  starting transfers between devices: 2.04 us -> 18.1 us
    all_gather x1 -> x0, waiting for transfers between devices: 66.3 us -> none  [on_device(): lax.all_gather(lookup_transform, 'seq', axis=0, tiled=True)]
    all_to_all x0 -> x1, starting transfers between devices: none -> 15.7 us  [on_device(): lax.all_to_all(jnp.stack([lookup_transform] * lax.axis_size('seq')), 'seq...]
    all_gather x1, waiting for transfers between devices: 35.5 us -> 23.3 us  [on_device(): lax.all_gather(current, 'mp', axis=1, tiled=True)]
    all_gather x1, waiting for transfers between devices: 64.6 us -> 71.8 us  [on_device(): lax.all_gather(acceptance_transform, 'seq', axis=0, tiled=True)]
where the time goes in v1:
time: 576 us; the launch traced here: 574 us
  waiting for transfers between devices  359 us (62%)
  other arithmetic  62.9 us (11%)
  blocking collectives  55.6 us (10%)
  local copies, waits for them, and re-layouts  33.2 us (6%)
  matrix products  29.1 us (5%)
  starting transfers between devices  18.1 us (3%)
  between operations  14.6 us (3%)
    reduce_scatter x1, waiting for transfers between devices, on_device(): lax.psum_scatter(jnp.dot(hidden, full_out, preferred_element_type=jnp.flo...  85.6 us
    all_gather x1, waiting for transfers between devices, on_device(): full_out = lax.all_gather(final_transform, 'seq', axis=1, tiled=True)  72.5 us
    all_gather x1, waiting for transfers between devices, on_device(): lax.all_gather(acceptance_transform, 'seq', axis=0, tiled=True)  71.8 us
    all_gather x1, waiting for transfers between devices, on_device(): lax.all_gather(payload_transform, 'seq', axis=0, tiled=True)  65.3 us
    all_gather x1, blocking collectives, entering(): pieces = jax.tree.map(lambda part: lax.all_gather(part, axis), value)  32.3 us
    select_n x31, other arithmetic, hop(): jnp.where(position < mine, new, old)  32 us
    all_gather x1, waiting for transfers between devices, entering(): pieces = jax.tree.map(lambda part: lax.all_gather(part, axis), value)  28.6 us
    all_gather x1, blocking collectives, on_device(): lax.all_gather(edge_row, 'mp', axis=1, tiled=True)  23.3 us
  transfers between devices with their start and end apart: 9, of which 8 were waited for; matrix products, arithmetic and copies ran while one was open for 16% of the time, Pallas kernels for 0%

profile of v1, /device:TPU:2, one launch (start us, length us, event | category | flops | bytes accessed | tf_op | source)
XLA Modules:
  0.0 573.8 jit_solution(14005594318898752000)
XLA Ops:
  7.2 1.6 pad_maximum_fusion.2
  9.6 2.4 stack.2
  12.0 15.7 %all-to-all-start = ((bf16[32,128,256]{2,1,0:T(8,128)(2,1)}), bf16[32,128,256]{2,1,0:T(8,128)(2,1)}, u32[]{:S(2)}, u32[]{:S(2)}) async-start(bf16[32,128,256]{2,1,0:T(8,128)(2,1)} %stack.2), calls=%async_computation | async-start | bytes 4194304 | tf_op jit(solution)/shard_map/all_to_all | solution.py:154
  29.3 2.1 collective-permute-start
  32.2 23.3 %all_gather.31 = bf16[1,4096]{1,0:T(2,128)(2,1)S(1)} all-gather(bf16[1,256]{1,0:T(2,128)(2,1)S(1)} %broadcast_select_fusion), channel_id=1, replica_groups=mesh['seq'=32,'mp'=16] {'mp'}, dimensions={1}, use_global_device_ids=true | all-gather | bytes 8704 | tf_op jit(solution)/shard_map/all_gather | solution.py:145
  55.5 23.3 %all-gather.8.cloned.1.call-done = bf16[256,4096]{1,0:T(8,128)(2,1)} async-done(((bf16[256,256]{1,0:T(8,128)(2,1)}), bf16[256,4096]{1,0:T(8,128)(2,1)}) %all-gather.8.cloned.1.call-update) | async-done | bytes 2097168 | tf_op jit(solution)/shard_map/all_gather | solution.py:144
  78.7 1.9 slice-done
  80.6 1.2 concatenate.24
  81.8 1.1 slice.99
  83.8 3.6 fusion.41
  87.4 2.2 slice_reduce_fusion
  90.5 71.8 %all-gather.12.cloned.1.call-done = bf16[4096,256]{1,0:T(8,128)(2,1)} async-done(((bf16[128,256]{1,0:T(8,128)(2,1)}), bf16[4096,256]{1,0:T(8,128)(2,1)}) %all-gather.12.cloned.1.call-update) | async-done | bytes 2097168 | tf_op jit(solution)/shard_map/all_gather | solution.py:152
  162.4 3.7 fusion.25
  167.6 65.3 %all-gather.10.cloned.1.call-done = bf16[4096,256]{1,0:T(8,128)(2,1)} async-done(((bf16[128,256]{1,0:T(8,128)(2,1)}), bf16[4096,256]{1,0:T(8,128)(2,1)}) %all-gather.10.cloned.1.call-update) | async-done | bytes 2097168 | tf_op jit(solution)/shard_map/all_gather | solution.py:157
  232.9 3.3 fusion.27
  237.8 3.3 fusion.29
  241.3 13.0 %while.29 = (s32[]{:T(128)}, f32[4,64,64]{2,1,0:T(8,128)S(1)}, f32[2,64,4,64]{1,0,3,2:T(2,128)}, f32[2,64,4,64]{1,0,3,2:T(2,128)}, f32[2,64,4,64]{3,2,1,0:T(4,12...) while((s32[]{:T(128)}, f32[4,64,64]{2,1,0:T(8,128)S(1)}, ...), condition=%wide.region_3.4_spmd.clone, body=%wide.region_0.3_spmd.clone.sunk | while | flops 51646208 | bytes 4017364 | solution.py:93
  241.4 1.4 constant_dynamic-slice_fusion.5
  244.4 2.8 dynamic_update_slice.6
  247.9 1.4 constant_dynamic-slice_fusion.5
  250.9 2.8 dynamic_update_slice.6
  257.1 32.3 %all_gather.35 = f32[32,4,64]{2,1,0:T(4,128)} all-gather(f32[1,4,64]{2,1,0:T(4,128)S(1)} %all_gather.34), channel_id=1, replica_groups=mesh['seq'=32,'mp'=16] {'seq'}, dimensions={0}, use_global_device_ids=true | all-gather | bytes 33792 | tf_op jit(solution)/shard_map/all_gather | solution.py:19
  292.0 1.1 exponential_multiply_fusion
  297.4 28.6 %all-gather.18.cloned.1.call-done = f32[128,64,64]{2,1,0:T(8,128)} async-done(((f32[4,64,64]{2,1,0:T(8,128)}), f32[128,64,64]{2,1,0:T(8,128)}) %all-gather.18.cloned.1.call-update) | async-done | bytes 2097168 | tf_op jit(solution)/shard_map/all_gather | solution.py:19
  326.1 53.9 %while.30 = (s32[]{:T(128)}, f32[4,64]{1,0:T(4,128)S(1)}, f32[4,64,64]{2,1,0:T(8,128)S(1)}, s32[]{:T(128)}, f32[32,4,64]{2,1,0:T(4,128)}, /*index=5*/f32[32,4,64,64]{3,2,1,0:T(8,128)}, s32[]{:T(128)}, s32[]{:T(128)}) while((s32[]{:T(128)}, f32[4,64]{1,0:T(4,128)S(1)}, f32[4,64,64]{2,1,0:T(8,128)S(1)}, s32[]{:T(128)}, ...), condition=%wide.region_6.7_spmd.clone, body=%wide.region_5.6_spmd.clone.sunk | while | flops 66308 | bytes 201843 | solution.py:28
  326.8 1.0 fusion.119
  328.5 1.0 fusion.119
  330.2 1.0 fusion.119
  331.9 1.0 fusion.119
  333.7 1.0 fusion.119
  335.4 1.0 fusion.119
  337.2 1.0 fusion.119
  338.9 1.0 fusion.119
  351.1 1.0 fusion.119
  352.8 1.0 fusion.119
  354.6 1.0 fusion.119
  368.5 1.0 fusion.119
  373.7 1.0 fusion.119
  375.5 1.0 fusion.119
  380.1 1.9 fusion.42
  382.8 1.8 copy.102
  385.3 1.8 copy.101
  387.2 9.4 %all-gather.14.cloned.1.call-done = bf16[4096,256]{1,0:T(8,128)(2,1)} async-done(((bf16[128,256]{1,0:T(8,128)(2,1)}), bf16[4096,256]{1,0:T(8,128)(2,1)}) %all-gather.14.cloned.1.call-update) | async-done | bytes 2097168 | tf_op jit(solution)/shard_map/all_gather | solution.py:158
  396.6 72.5 %all-gather.16.cloned.1.call-done = bf16[256,4096]{1,0:T(8,128)(2,1)} async-done(((bf16[256,128]{1,0:T(8,128)(2,1)}), bf16[256,4096]{1,0:T(8,128)(2,1)}) %all-gather.16.cloned.1.call-update) | async-done | bytes 2097168 | tf_op jit(solution)/shard_map/all_gather | solution.py:237
  469.1 7.5 %fusion.63 = f32[256,4096]{1,0:T(8,128)} fusion(bf16[256,4096]{1,0:T(8,128)(2,1)} %all-gather.16.cloned.1.call-done, f32[256,256]{1,0:T(8,128)} %copy.102, f32[256,256]{1,0:T(8,128)} %copy.101, f32[128,256]{1,0:T(8,128)} %concatenate.27, f32[128,256]{1,0:T(8,128)S(1)} %copy.99, bf16[4096,256]{1,0:T(8,128)(2,1)} %all-gather.14.cloned.1.call-done, ...), kind=kOutput, calls=%fused_computation.83 | convolution fusion | flops 1086062592 | bytes 13388032 | tf_op jit(solution)/shard_map/dot_general | solution.py:239
  477.6 1.3 convolution_add_fusion.1
  479.7 85.6 %reduce-scatter.2.cloned.1.call-done = f32[16,4096]{1,0:T(8,128)} async-done(((f32[256,4096]{1,0:T(8,128)}), f32[16,4096]{1,0:T(8,128)}) %reduce-scatter.2.cloned.1.call-update) | async-done | bytes 262160 | tf_op jit(solution)/shard_map/reduce_scatter | solution.py:238
  565.3 1.6 convert_bitcast_fusion
  (213 shorter events, 64.1 us)
Async XLA Ops:
  7.2 75.8 %copy-start = (bf16[4096,128]{1,0:T(8,128)(2,1)S(1)}, bf16[4096,128]{1,0:T(8,128)(2,1)}, u32[]{:S(2)}) copy-start(bf16[4096,128]{1,0:T(8,128)(2,1)} %param.32) | copy-start | bytes 3145732
  7.2 71.5 %all-gather.8.cloned.1.call-start = ((), (), s32[]{:S(2)}) async-start(), calls=%async_computation.2 | async-start | bytes 2228224 | tf_op jit(solution)/shard_map/all_gather | solution.py:144
  8.9 153.5 %all-gather.12.cloned.1.call-start = ((), (), s32[]{:S(2)}) async-start(), calls=%async_computation.4 | async-start | bytes 2162688 | tf_op jit(solution)/shard_map/all_gather | solution.py:152
  12.0 19.3 %copy-start.23 = (f32[5,4096]{1,0:T(8,128)S(1)}, f32[5,4096]{1,0:T(8,128)}, u32[]{:S(2)}) copy-start(f32[5,4096]{1,0:T(8,128)} %param.26) | copy-start | bytes 245764
  12.0 20.1 %copy-start.26 = (bf16[256]{0:T(256)(128)(2,1)S(1)}, bf16[256]{0:T(256)(128)(2,1)}, u32[]{:S(2)}) copy-start(bf16[256]{0:T(256)(128)(2,1)} %param.24) | copy-start | bytes 1540
  12.0 225.7 %all-to-all-start = ((bf16[32,128,256]{2,1,0:T(8,128)(2,1)}), bf16[32,128,256]{2,1,0:T(8,128)(2,1)}, u32[]{:S(2)}, u32[]{:S(2)}) async-start(bf16[32,128,256]{2,1,0:T(8,128)(2,1)} %stack.2), calls=%async_computation | async-start | bytes 4194304 | tf_op jit(solution)/shard_map/all_to_all | solution.py:154
  27.8 205.1 %all-gather.10.cloned.1.call-start = ((), (), s32[]{:S(2)}) async-start(), calls=%async_computation.3 | async-start | bytes 2162688 | tf_op jit(solution)/shard_map/all_gather | solution.py:157
  28.5 297.6 %all-gather.18.cloned.1.call-start = ((), (), s32[]{:S(2)}) async-start(), calls=%async_computation.8 | async-start | bytes 4325376 | tf_op jit(solution)/shard_map/all_gather | solution.py:19
  29.3 2.9 collective-permute-start
  55.5 106.9 %copy-start.24 = (bf16[1,4096]{1,0:T(2,128)(2,1)}, bf16[1,4096]{1,0:T(2,128)(2,1)S(1)}, u32[]{:S(2)}) copy-start(bf16[1,4096]{1,0:T(2,128)(2,1)S(1)} %all_gather.31) | copy-start | bytes 24580
  78.7 1.9 slice-start
  78.7 3.1 copy-start.3
  80.6 2.4 copy-start.28
  80.6 2.4 copy-start.29
  81.8 2.0 copy-start.4
  89.7 76.4 %copy-start.9 = (f32[128,256]{0,1:T(8,128)}, f32[128,256]{0,1:T(8,128)S(1)}, u32[]{:S(2)}) copy-start(f32[128,256]{0,1:T(8,128)S(1)} %get-tuple-element.274) | copy-start | bytes 393220
  166.7 69.5 %copy-start.11 = (f32[128,256]{0,1:T(8,128)}, f32[128,256]{0,1:T(8,128)S(1)}, u32[]{:S(2)}) copy-start(f32[128,256]{0,1:T(8,128)S(1)} %get-tuple-element.275) | copy-start | bytes 393220
  237.8 3.5 copy-start.22
  241.3 15.0 %copy-start.27 = (s32[2]{0:T(128)S(1)}, s32[2]{0:T(128)}, u32[]{:S(2)}) copy-start(s32[2]{0:T(128)} %param.23) | copy-start | bytes 28
  241.3 15.7 %copy-start.25 = (f32[256]{0:T(256)S(1)}, f32[256]{0:T(256)}, u32[]{:S(2)}) copy-start(f32[256]{0:T(256)} %get-tuple-element.272) | copy-start | bytes 3076
  241.3 48.1 %copy-start.10 = (f32[128,256]{0,1:T(8,128)S(1)}, f32[128,256]{0,1:T(8,128)}, u32[]{:S(2)}) copy-start(f32[128,256]{0,1:T(8,128)} %copy-done.9) | copy-start | bytes 393220
  241.3 48.2 %copy-start.15 = (f32[128,256]{0,1:T(8,128)S(1)}, f32[128,256]{0,1:T(8,128)}, u32[]{:S(2)}) copy-start(f32[128,256]{0,1:T(8,128)} %get-tuple-element.273) | copy-start | bytes 393220
  241.4 2.6 copy-start.6
  241.4 3.0 copy-start.19
  247.2 0.7 copy-start.20
  247.9 2.6 copy-start.6
  247.9 3.0 copy-start.19
  253.6 0.7 copy-start.20
  254.3 0.7 copy-start.1
  254.3 35.8 %copy-start.12 = (f32[128,256]{0,1:T(8,128)S(1)}, f32[128,256]{0,1:T(8,128)}, u32[]{:S(2)}) copy-start(f32[128,256]{0,1:T(8,128)} %copy-done.11) | copy-start | bytes 393220
  254.3 36.0 %copy-start.16 = (f32[128,256]{0,1:T(8,128)S(1)}, f32[128,256]{0,1:T(8,128)}, u32[]{:S(2)}) copy-start(f32[128,256]{0,1:T(8,128)} %get-tuple-element.276) | copy-start | bytes 393220
  254.3 36.3 %copy-start.17 = (f32[128,256]{1,0:T(8,128)S(1)}, f32[128,256]{1,0:T(8,128)}, u32[]{:S(2)}) copy-start(f32[128,256]{1,0:T(8,128)} %get-tuple-element.278) | copy-start | bytes 393220
  255.0 141.6 %all-gather.14.cloned.1.call-start = ((), (), s32[]{:S(2)}) async-start(), calls=%async_computation.5 | async-start | bytes 2162688 | tf_op jit(solution)/shard_map/all_gather | solution.py:158
  255.6 213.5 %all-gather.16.cloned.1.call-start = ((), (), s32[]{:S(2)}) async-start(), calls=%async_computation.6 | async-start | bytes 2162688 | tf_op jit(solution)/shard_map/all_gather | solution.py:237
  256.2 309.1 %reduce-scatter.2.cloned.1.call-start = ((), (), s32[]{:S(2)}) async-start(), calls=%async_computation.7 | async-start | bytes 4456448 | tf_op jit(solution)/shard_map/reduce_scatter | solution.py:238
  290.1 3.0 copy-start.13
  291.0 2.8 copy-start.7
  293.1 2.4 copy-start.21
  380.0 89.1 %copy-start.5 = (bf16[256,4096]{1,0:T(8,128)(2,1)S(1)}, bf16[256,4096]{1,0:T(8,128)(2,1)}, u32[]{:S(2)}) copy-start(bf16[256,4096]{1,0:T(8,128)(2,1)} %all-gather.8.cloned.1.call-done) | copy-start | bytes 6291460
  380.0 89.1 %copy-start.30 = (f32[256]{0:T(256)S(1)}, f32[256]{0:T(256)}, u32[]{:S(2)}) copy-start(f32[256]{0:T(256)} %param.36) | copy-start | bytes 3076
  476.6 0.9 copy-start.8
  476.6 1.0 copy-start.14
  476.6 2.3 copy-start.2
  476.6 2.3 copy-start.18
Sparse Core Ops, SparseCore 0:
  11.6 67.1 all-gather.7
  80.8 81.4 all-gather.11
  164.5 68.3 all-gather.9
  255.1 70.8 all-gather.17
  328.0 68.4 all-gather.13
  398.5 70.5 all-gather.15
  476.8 88.5 reduce-scatter.1
